TPU v7x, 256 devices: a whole 4x4x8 slice. The times are simulated.
256 devices in a mesh: samp: 8 (over y, core), par: 32 (over z, x).
Axes of the slice: x: 4, y: 4, z: 8, core: 2. Of those that a mesh axis runs over, the one named last changes fastest.
Arguments:
- jacobian: bfloat16 [8192, 65536], P(('samp', 'par')), as said below
- sample_slot: int32 [8192], P(('samp', 'par')), may hold values from 0 to 1023, as said below
- panel_index: int32 [1], replicated, may hold values from 0 to 8191
- shift_value: float32 [1], replicated, may hold values from 0.1 to 1
Outputs:
- cholesky_panel: float32 [8192, 1024], P(('samp', 'par'))
Inputs may be any that keep to these rules, and one draw needn't show every extreme that they name: Within each group (samples g * 1024 to (g + 1) * 1024 - 1), sample_slot is a permutation of 0 to 1023. `jacobian`: finite values.
All inputs are finite; a program needn't handle non-finite values.
Results may differ from a plain program's by a relative error of at most 0.0003.
Values may be sent and summed in bfloat16 or wider, within the bound.
A program may use at most 128 MiB of HBM per device.

v0:
```python
import functools

import jax
import jax.numpy as jnp
from jax import lax
from jax.experimental import pallas as pl
from jax.experimental.pallas import tpu as pltpu
from jax.sharding import Mesh
from jax.sharding import PartitionSpec as P

PAR = ("z", "x")
PLANE = ("samp", "x")
ALL = ("samp", "z", "x")
NB = 128
STEP = 16
HI = lax.Precision.HIGHEST


def rank_update(r):
    h = r.astype(jnp.bfloat16).astype(jnp.float32)
    m = (r - h).astype(jnp.bfloat16).astype(jnp.float32)
    l = (r - h - m).astype(jnp.bfloat16).astype(jnp.float32)
    lhs = jnp.concatenate([h, h, m, h, l, m], 0).astype(jnp.bfloat16)
    rhs = jnp.concatenate([h, m, h, l, h, m], 0).astype(jnp.bfloat16)
    return lax.dot_general(
        lhs, rhs, (((0,), (0,)), ((), ())), preferred_element_type=jnp.float32
    )


def inverse_of_factor(block, filler):
    n = block.shape[0]
    groups = n // STEP
    rows = [block[STEP * i : STEP * i + STEP, :] for i in range(groups)]
    sub = lax.broadcasted_iota(jnp.int32, (STEP, n), 0)
    lane = lax.broadcasted_iota(jnp.int32, (STEP, n), 1)
    for b in range(groups):
        first = STEP * b
        r = rows[b]
        cols = [jnp.broadcast_to(r[:, first + j : first + j + 1], (STEP, n)) for j in range(STEP)]
        inside = (lane >= first) & (lane < first + STEP)
        r = jnp.where(inside, jnp.where(lane == sub + first, 1.0, 0.0), r)
        diag = jnp.ones((STEP, n), jnp.float32)
        for j in range(STEP):
            d = jnp.broadcast_to(cols[j][j : j + 1, :], (8, n))
            diag = jnp.where(sub == j, jnp.concatenate([d] * (STEP // 8), 0), diag)
            if j == STEP - 1:
                break
            low = (j + 1) // 8 * 8
            below = (STEP - low) // 8
            q = pl.reciprocal(d, approx=True)
            e = jnp.concatenate([1.0 - d * q] * below, 0)
            m = jnp.where(sub[low:] > j, cols[j][low:], 0.0) * jnp.concatenate([q] * below, 0)
            m = m + m * e

            def eliminated(v):
                left = v[low:] - m * jnp.broadcast_to(v[j : j + 1, :], (STEP - low, n))
                return left if low == 0 else jnp.concatenate([v[:low], left], 0)

            for c in range(j + 1, STEP):
                cols[c] = eliminated(cols[c])
            r = eliminated(r)
        s = lax.rsqrt(diag)
        s = s * (1.5 - 0.5 * diag * s * s)
        r = r * s
        rows[b] = r
        if b < groups - 1:
            p = rank_update(r)
            for i in range(b + 1, groups):
                rows[i] = jnp.where(inside, 0.0, rows[i]) - p[STEP * i : STEP * i + STEP, :]
        filler()
    kept = [jnp.where(lane <= sub + STEP * b, rows[b], 0.0) for b in range(groups)]
    return jnp.concatenate(kept, 0)


def times_transposed(a, b):
    return lax.dot_general(
        a, b, (((1,), (1,)), ((), ())), precision=HI, preferred_element_type=jnp.float32
    )


def factor_kernel(a_ref, g_ref, x_ref, o_ref):
    n = a_ref.shape[0]
    steps = n // NB
    waiting = []

    def run(count):
        for _ in range(min(count, len(waiting))):
            waiting.pop(0)()

    x_ref[...] = g_ref[...]
    for kb in range(steps):
        s_ref = a_ref if kb == 0 else o_ref
        own = slice(kb * NB, kb * NB + NB)
        share = -(-len(waiting) // (NB // STEP))
        w = inverse_of_factor(s_ref[own, own], lambda: run(share))
        run(len(waiting))
        lo = (kb + 1) * NB
        x_ref[:, own] = times_transposed(x_ref[:, own], w)
        if kb == steps - 1:
            break
        o_ref[lo:, own] = times_transposed(s_ref[lo:, own], w)

        def update(j, top, end, s_ref=s_ref, own=own):
            cj = slice(j * NB, j * NB + NB)
            o_ref[top:end, cj] = s_ref[top:end, cj] - times_transposed(
                o_ref[top:end, own], o_ref[cj, own]
            )

        def advance(left, end, own=own):
            x_ref[:, left:end] = x_ref[:, left:end] - times_transposed(
                x_ref[:, own], o_ref[left:end, own]
            )

        update(kb + 1, lo, n)
        waiting.append(functools.partial(advance, lo, n))
        for j in range(kb + 2, steps):
            for top in range(j * NB, n, 2 * NB):
                waiting.append(functools.partial(update, j, top, min(n, top + 2 * NB)))


def solved(rows, block):
    vmem = pl.BlockSpec(memory_space=pltpu.VMEM)
    return pl.pallas_call(
        factor_kernel,
        out_shape=jax.ShapeDtypeStruct(rows.shape, jnp.float32),
        in_specs=[vmem, vmem],
        out_specs=vmem,
        scratch_shapes=[pltpu.VMEM(block.shape, jnp.float32)],
        name="factor",
    )(block, rows)


MESH_IDS = pl.DeviceIdType.MESH
Z, X, Y, GROUPS = 8, 4, 4, 8
CHUNKS = 8
SAMPLES = 8192
LEAD = 2


def here():
    samp, z, x = lax.axis_index("samp"), lax.axis_index("z"), lax.axis_index("x")
    return samp, z, x


def wrapped(value, size):
    return lax.rem(value + size, size)


def meet(peers):
    barrier = pltpu.get_barrier_semaphore()
    for peer in peers:
        pl.semaphore_signal(barrier, inc=1, device_id=peer, device_id_type=MESH_IDS)
    pl.semaphore_wait(barrier, len(peers))


def at(samp, z, x):
    return {"samp": samp, "z": z, "x": x}


def plane_peers(samp, z, x):
    return [
        (ds, dx, at(wrapped(samp + ds, GROUPS), z, wrapped(x + dx, X)))
        for ds in range(GROUPS)
        for dx in range(X)
        if (ds, dx) != (0, 0)
    ]


def column_peers(samp, z, x):
    return [(dz, at(samp, wrapped(z + dz, Z), x)) for dz in range(1, Z)]


def copy_to(src, dst, send, recv, peer):
    return pltpu.make_async_remote_copy(
        src_ref=src, dst_ref=dst, send_sem=send, recv_sem=recv,
        device_id=peer, device_id_type=MESH_IDS,
    )


def exchange_kernel(jac_ref, slot_ref, place_ref, c_ref, p_ref, slots_ref,
                    tile_ref, pivot_ref, near, matched, ordered,
                    own_sem, send, recv, zsend, zrecv, ps, pr, zs, zr):
    samp, z, x = here()
    right, left = wrapped(z + 1, Z), wrapped(z - 1, Z)
    column, plane = column_peers(samp, z, x), plane_peers(samp, z, x)
    me = at(samp, z, x)
    meet([peer for _, peer in column] + [peer for _, _, peer in plane])
    wide = tile_ref.shape[-1]
    n = ordered.shape[0]
    others = GROUPS * X - 1
    sends = []

    def start(copy):
        copy.start()
        sends.append(copy)

    def arrived(ref, send_sem, recv_sem):
        copy_to(ref, ref, send_sem, recv_sem, me).wait_recv()

    def columns(s, u, q):
        first = pl.multiple_of(((s * X + u) * CHUNKS + q) * wide, wide)
        return jac_ref.at[:, pl.ds(first, wide)]

    def within(q, i):
        turn = lax.rem(7 * i, others) + 1
        ds, dx = turn // X, lax.rem(turn, X)
        s, u = wrapped(samp + ds, GROUPS), wrapped(x + dx, X)
        return copy_to(columns(s, u, q), tile_ref.at[q, samp, x],
                       send.at[q, ds, dx], recv.at[q, ds, dx], at(s, z, u))

    def issue(q, begin, end):
        @pl.when(q < CHUNKS)
        def _():
            @pl.loop(begin, end)
            def _(i):
                within(q, i).start()

    def landed(q):
        @pl.loop(1, others + 1)
        def _(turn):
            ds, dx = turn // X, lax.rem(turn, X)
            arrived(tile_ref.at[q, wrapped(samp - ds, GROUPS), wrapped(x - dx, X)],
                    send.at[q, ds, dx], recv.at[q, ds, dx])

    def own_copy(q):
        return pltpu.make_async_copy(columns(samp, x, q), tile_ref.at[q, samp, x], own_sem.at[q])

    def hop_copy(d, s, q):
        owner = wrapped(z - s, Z) if d == 0 else wrapped(z + s, Z)
        ref = pivot_ref.at[q, owner]
        return copy_to(ref, ref, zsend.at[d, s, q], zrecv.at[d, s, q],
                       at(samp, right if d == 0 else left, x))

    def came(d, s, q):
        owner = wrapped(z - 1 - s, Z) if d == 0 else wrapped(z + 1 + s, Z)
        arrived(pivot_ref.at[q, owner], zsend.at[d, s, q], zrecv.at[d, s, q])

    near[samp, x] = slot_ref[...]
    for ds, dx, peer in plane:
        start(copy_to(slot_ref, near.at[samp, x], ps.at[ds, dx], pr.at[ds, dx], peer))
    for q in range(CHUNKS):
        own_copy(q).start()
    for q in range(LEAD):
        issue(q, 0, others)

    for ds, dx, _ in plane:
        arrived(near.at[wrapped(samp - ds, GROUPS), wrapped(x - dx, X)],
                ps.at[ds, dx], pr.at[ds, dx])
    row = lax.broadcasted_iota(jnp.int32, (GROUPS, 128), 0)
    joined = jnp.zeros((GROUPS, 128), jnp.int32)
    for g in range(GROUPS):
        line = near[g, 0] + near[g, 1] + near[g, 2] + near[g, 3]
        joined = jnp.where(row == g, line, joined)
    slots_ref[z] = joined
    for dz, peer in column:
        ref = slots_ref.at[z]
        start(copy_to(ref, ref, zs.at[dz], zr.at[dz], peer))
    c_ref[...] = jnp.zeros_like(c_ref)
    p_ref[...] = jnp.zeros_like(p_ref)
    for dz, _ in column:
        arrived(slots_ref.at[wrapped(z - dz, Z)], zs.at[dz], zr.at[dz])
    wanted = lax.rem(lax.broadcasted_iota(jnp.int32, (n, 128), 0) + place_ref[1], n)
    for v in range(Z):
        line = jnp.sum(jnp.where(row == place_ref[0], slots_ref[v], 0), axis=0, keepdims=True)
        matched[:, v * 128 : v * 128 + 128] = jnp.where(wanted == line, 1.0, 0.0).astype(jnp.bfloat16)

    def products(q):
        part = n // 4
        raw = pivot_ref[q].reshape(n, wide)
        for i in range(4):
            ordered[i * part : i * part + part, :] = jnp.dot(
                matched[i * part : i * part + part, :], raw, preferred_element_type=jnp.float32
            ).astype(jnp.bfloat16)
        contract = (((1,), (1,)), ((), ()))
        whole = ordered[...]
        for i in range(Y):
            rows = tile_ref[q, 2 * i : 2 * i + 2].reshape(-1, wide)
            c_ref[i] = c_ref[i] + lax.dot_general(
                rows, whole, contract, preferred_element_type=jnp.float32
            ).reshape(c_ref.shape[1:])
        band = ordered[pl.ds(pl.multiple_of(z * 128, 128), 128), :]
        p_ref[...] = p_ref[...] + lax.dot_general(
            band, whole, contract, preferred_element_type=jnp.float32
        ).reshape(p_ref.shape)

    @pl.loop(0, CHUNKS + 4)
    def _(tick):
        @pl.when(tick < CHUNKS)
        def _():
            landed(tick)
            own_copy(tick).wait()
            picked = tile_ref[tick, 0]
            for g in range(1, GROUPS):
                picked = jnp.where(place_ref[0] == g, tile_ref[tick, g], picked)
            pivot_ref[tick, z] = picked
            for d in range(2):
                hop_copy(d, 0, tick).start()

        issue(tick + LEAD, 0, 8)
        for s in range(1, 4):
            q = tick - s

            @pl.when((q >= 0) & (q < CHUNKS))
            def _():
                for d in range(2):
                    came(d, s - 1, q)
                    if s < 3:
                        hop_copy(d, s, q).start()
                    else:
                        @pl.when(lax.rem(q, 2) == d)
                        def _():
                            hop_copy(d, s, q).start()

            issue(tick + LEAD, 8 * s, min(8 * s + 8, others))

        @pl.when(tick >= 4)
        def _():
            q = tick - 4
            for d in range(2):
                @pl.when(lax.rem(q, 2) == d)
                def _():
                    came(d, 3, q)
            products(q)

    @pl.loop(0, CHUNKS)
    def _(q):
        @pl.loop(0, others)
        def _(i):
            within(q, i).wait_send()
        for d in range(2):
            for s in range(3):
                hop_copy(d, s, q).wait_send()

            @pl.when(lax.rem(q, 2) == d)
            def _():
                hop_copy(d, 3, q).wait_send()

    for copy in sends:
        copy.wait_send()


def exchanged(jacobian, slots, place):
    vmem = pl.BlockSpec(memory_space=pltpu.VMEM)
    dma = pltpu.SemaphoreType.DMA
    rows, params = jacobian.shape
    wide = params // (GROUPS * X * CHUNKS)
    n = Z * X * rows
    f32, bf16 = jnp.float32, jnp.bfloat16
    return pl.pallas_call(
        exchange_kernel,
        out_shape=(
            jax.ShapeDtypeStruct((Y, 2, X, rows, n), f32),
            jax.ShapeDtypeStruct((Y, 2, 2, 8, n), f32),
            jax.ShapeDtypeStruct((Z, GROUPS, 128), slots.dtype),
        ),
        in_specs=[pl.BlockSpec(memory_space=pl.ANY), vmem,
                  pl.BlockSpec(memory_space=pltpu.SMEM)],
        out_specs=(vmem, vmem, vmem),
        scratch_shapes=[pltpu.VMEM((CHUNKS, GROUPS, X, rows, wide), bf16),
                        pltpu.VMEM((CHUNKS, Z, X, rows, wide), bf16),
                        pltpu.VMEM((GROUPS, X, 1, 128), slots.dtype),
                        pltpu.VMEM((n, n), bf16), pltpu.VMEM((n, wide), bf16),
                        dma((CHUNKS,)), dma((CHUNKS, GROUPS, X)), dma((CHUNKS, GROUPS, X)),
                        dma((2, 4, CHUNKS)), dma((2, 4, CHUNKS)),
                        dma((GROUPS, X)), dma((GROUPS, X)), dma((Z,)), dma((Z,))],
        compiler_params=pltpu.CompilerParams(collective_id=0, has_side_effects=True),
        name="exchange",
    )(jacobian, slots, place)


def reduce_kernel(p_ref, c_ref, pick_ref, place_ref, shift_ref, o_ref, g_ref,
                  got, piece, sib, acc, first0, first1, acc0, acc1, second0, second1,
                  part, column_rows, chosen, third,
                  ps, pr, zs, zr, xs, xr, ys, yr, ys2, yr2, xs2, xr2, cs, cr,
                  ss, sr, s0, r0, s1, r1, t0, q0, t1, q1, us, ur, vs, vr):
    samp, z, x = here()
    y, core = samp // 2, lax.rem(samp, 2)
    xh, xl = x // 2, lax.rem(x, 2)
    me, sibling = at(samp, z, x), at(2 * y + 1 - core, z, x)
    column, plane = column_peers(samp, z, x), plane_peers(samp, z, x)
    meet([peer for _, peer in column] + [peer for _, _, peer in plane])
    n = p_ref.shape[4]
    wide = n // 2
    low, high = pl.ds(0, wide), pl.ds(wide, wide)
    order = (2, 1, 3)
    sends = []

    def start(copy):
        copy.start()
        sends.append(copy)

    def arrived(ref, send, recv):
        copy_to(ref, ref, send, recv, me).wait_recv()

    def cols(xlow, color=None):
        if color is None:
            return pl.ds(pl.multiple_of(xlow * wide, wide), wide)
        return pl.ds(pl.multiple_of(xlow * wide + color * (wide // 2), wide // 2), wide // 2)

    def up(d):
        v = wrapped(y + d, Y)
        return v, at(2 * v + core, z, x)

    def along(d):
        u = wrapped(x + d, X)
        return u, at(samp, z, u)

    for ds, dx, peer in plane:
        s, u = wrapped(samp + ds, GROUPS), wrapped(x + dx, X)
        start(copy_to(p_ref.at[s // 2, lax.rem(s, 2), u // 2, :, cols(lax.rem(u, 2))],
                      got.at[ds, dx], ps.at[ds, dx], pr.at[ds, dx], peer))
    for d in order + (0,):
        v, _ = up(d)
        start(copy_to(c_ref.at[v, 1 - core], sib.at[v], ss.at[d], sr.at[d], sibling))
    for d in order + (0,):
        v, peer = up(d)
        arrived(sib.at[v], ss.at[d], sr.at[d])
        acc[v] = c_ref[v, core] + sib[v]
        if d:
            start(copy_to(acc.at[v, :, :, low], first0.at[d], s0.at[d], r0.at[d], peer))
    for d in order:
        u, peer = along(d)
        start(copy_to(acc.at[:, u, :, high], first1.at[d], s1.at[d], r1.at[d], peer))

    total = p_ref[y, core, xh, :, cols(xl)]
    for ds, dx, _ in plane:
        arrived(got.at[ds, dx], ps.at[ds, dx], pr.at[ds, dx])
    for ds, dx, _ in plane:
        total = total + got[ds, dx]
    shape = total.shape
    row = lax.broadcasted_iota(jnp.int32, shape, 0) + (z * 128 + (2 * samp + xh) * 8)
    column_id = lax.broadcasted_iota(jnp.int32, shape, 1) + xl * wide
    total = total / SAMPLES + jnp.where(row == column_id, shift_ref[0], 0.0)
    piece[...] = total
    o_ref[z, y, core, xh, :, cols(xl)] = total
    for dz, peer in column:
        start(copy_to(piece, o_ref.at[z, y, core, xh, :, cols(xl)], zs.at[dz], zr.at[dz], peer))
    for dz, _ in column:
        arrived(o_ref.at[wrapped(z - dz, Z), y, core, xh, :, cols(xl)], zs.at[dz], zr.at[dz])
    for d in order:
        ref0 = o_ref.at[:, y, core, xh, :, cols(xl, 0)]
        start(copy_to(ref0, ref0, xs.at[d], xr.at[d], along(d)[1]))
        ref1 = o_ref.at[:, y, core, xh, :, cols(xl, 1)]
        start(copy_to(ref1, ref1, ys.at[d], yr.at[d], up(d)[1]))

    for d in order:
        arrived(first0.at[d], s0.at[d], r0.at[d])
    acc0[...] = acc[y, :, :, low] + first0[1] + first0[2] + first0[3]
    for d in order:
        u, peer = along(d)
        start(copy_to(acc0.at[u], second0.at[d], t0.at[d], q0.at[d], peer))
    for d in order:
        arrived(first1.at[d], s1.at[d], r1.at[d])
    acc1[...] = acc[:, x, :, high] + first1[1] + first1[2] + first1[3]
    for d in order:
        v, peer = up(d)
        start(copy_to(acc1.at[v], second1.at[d], t1.at[d], q1.at[d], peer))

    for d in order:
        u = wrapped(x - d, X)
        arrived(o_ref.at[:, y, core, u // 2, :, cols(lax.rem(u, 2), 0)], xs.at[d], xr.at[d])
    for d in order:
        for half in range(2):
            ref = o_ref.at[:, y, core, :, :, cols(half, 0)]
            start(copy_to(ref, ref, ys2.at[d, half], yr2.at[d, half], up(d)[1]))
    for d in order:
        v = wrapped(y - d, Y)
        arrived(o_ref.at[:, v, core, xh, :, cols(xl, 1)], ys.at[d], yr.at[d])
    for d in order:
        ref = o_ref.at[:, :, core, xh, :, cols(xl, 1)]
        start(copy_to(ref, ref, xs2.at[d], xr2.at[d], along(d)[1]))

    for d in order:
        arrived(second0.at[d], t0.at[d], q0.at[d])
        arrived(second1.at[d], t1.at[d], q1.at[d])
    part[:, low] = acc0[x] + second0[1] + second0[2] + second0[3]
    part[:, high] = acc1[y] + second1[1] + second1[2] + second1[3]
    column_rows[z] = part[...]
    for dz, peer in column:
        start(copy_to(part, column_rows.at[z], us.at[dz], ur.at[dz], peer))

    for d in order:
        u = wrapped(x - d, X)
        arrived(o_ref.at[:, :, core, u // 2, :, cols(lax.rem(u, 2), 1)], xs2.at[d], xr2.at[d])
    for d in (0,) + order:
        v = wrapped(y - d, Y)
        if d:
            for half in range(2):
                arrived(o_ref.at[:, v, core, :, :, cols(half, 0)], ys2.at[d, half], yr2.at[d, half])
        ref = o_ref.at[:, v, core]
        start(copy_to(ref, ref, cs.at[d], cr.at[d], sibling))

    for dz, _ in column:
        arrived(column_rows.at[wrapped(z - dz, Z)], us.at[dz], ur.at[dz])
    rest = column_rows[...].reshape(pick_ref.shape[1], n)
    moved = jnp.zeros((pick_ref.shape[0], n), jnp.float32)
    for _ in range(3):
        head = rest.astype(jnp.bfloat16)
        rest = rest - head.astype(jnp.float32)
        moved = moved + lax.dot_general(
            pick_ref[...], head, (((1,), (0,)), ((), ())), preferred_element_type=jnp.float32
        )
    chosen[...] = moved.reshape(chosen.shape)
    for d in order:
        u, peer = along(d)
        start(copy_to(chosen.at[u], third.at[d], vs.at[d], vr.at[d], peer))
    width = chosen.shape[1]
    position = lax.broadcasted_iota(jnp.int32, (width, n), 0) + (z * X + x) * width
    column_id = lax.broadcasted_iota(jnp.int32, (width, n), 1)
    on_pivot = jnp.where(position == lax.rem(column_id + place_ref[1], n), shift_ref[0], 0.0)
    on_pivot = jnp.where(place_ref[0] == samp, on_pivot, 0.0)
    for d in order:
        arrived(third.at[d], vs.at[d], vr.at[d])
    g_ref[...] = (chosen[x] + third[1] + third[2] + third[3]) / SAMPLES + on_pivot
    for d in range(Y):
        arrived(o_ref.at[:, wrapped(y - d, Y), 1 - core], cs.at[d], cr.at[d])
    for copy in sends:
        copy.wait_send()


def reduced(part, partial, pick, place, shift):
    vmem = pl.BlockSpec(memory_space=pltpu.VMEM)
    smem = pl.BlockSpec(memory_space=pltpu.SMEM)
    dma = pltpu.SemaphoreType.DMA
    rows, n = partial.shape[3:]
    wide = n // 2
    f32 = jnp.float32
    block, my_rows = pl.pallas_call(
        reduce_kernel,
        out_shape=(jax.ShapeDtypeStruct((Z, Y, 2, 2, 8, n), f32),
                   jax.ShapeDtypeStruct((rows, n), f32)),
        in_specs=[vmem, vmem, vmem, smem, smem],
        out_specs=(vmem, vmem),
        scratch_shapes=[
            pltpu.VMEM((GROUPS, X, 8, wide), f32), pltpu.VMEM((8, wide), f32),
            pltpu.VMEM((Y, X, rows, n), f32), pltpu.VMEM((Y, X, rows, n), f32),
            pltpu.VMEM((Y, X, rows, wide), f32), pltpu.VMEM((X, Y, rows, wide), f32),
            pltpu.VMEM((X, rows, wide), f32), pltpu.VMEM((Y, rows, wide), f32),
            pltpu.VMEM((X, rows, wide), f32), pltpu.VMEM((Y, rows, wide), f32),
            pltpu.VMEM((rows, n), f32), pltpu.VMEM((Z, rows, n), f32),
            pltpu.VMEM((X, rows, n), f32), pltpu.VMEM((X, rows, n), f32),
            dma((GROUPS, X)), dma((GROUPS, X)), dma((Z,)), dma((Z,)),
            dma((4,)), dma((4,)), dma((4,)), dma((4,)),
            dma((4, 2)), dma((4, 2)), dma((4,)), dma((4,)), dma((4,)), dma((4,)),
        ] + [dma((4,))] * 10 + [dma((Z,)), dma((Z,)), dma((4,)), dma((4,))],
        compiler_params=pltpu.CompilerParams(collective_id=1, has_side_effects=True),
        name="reduce",
    )(part, partial, pick, place, shift)
    return block.reshape(n, n), my_rows


def on_device(jacobian, sample_slot, panel_index, shift_value):
    width = sample_slot.shape[0]
    group_width = width * lax.axis_size(PAR)
    pivot_group = panel_index[0] // group_width
    rotation = panel_index[0] % group_width
    band = group_width // lax.axis_size("z")
    lanes = jnp.tile(sample_slot, X).reshape(1, width * X)
    own_lanes = jnp.arange(width * X, dtype=jnp.int32)[None, :] // width == lax.axis_index("x")
    padded = jnp.where(own_lanes, lanes, 0)
    place = jnp.stack([pivot_group, rotation])
    partial, pivot_part, slots = exchanged(jacobian, padded, place)
    own_slots = lax.dynamic_index_in_dim(slots, lax.axis_index("samp"), 1, keepdims=False)
    sources = own_slots.reshape(-1, X, width)
    sources = lax.dynamic_index_in_dim(sources, lax.axis_index("x"), 1, keepdims=False)
    target = lax.axis_index("z") * band + jnp.arange(band, dtype=jnp.int32)
    pick = (target[:, None] == sources.reshape(1, -1)).astype(jnp.bfloat16)
    block, my_rows = reduced(pivot_part, partial, pick, place, shift_value)
    return solved(my_rows, block)


def solution(mesh):
    torus = Mesh(mesh.devices.reshape(mesh.shape["samp"], 8, 4), ("samp", "z", "x"))
    return jax.shard_map(
        on_device,
        mesh=torus,
        in_specs=(P(ALL, None), P(ALL), P(), P()),
        out_specs=P(ALL, None),
        check_vma=False,
    )
```

profile of v0, /device:TPU:2, one launch (start us, length us, event | category | flops | bytes accessed | tf_op | source)
XLA Modules:
  0.0 215.0 jit_solution(6017178210780196205)
XLA Ops:
  1.3 0.7 pad_add_fusion.place_ref
  2.0 0.7 tile.2
  2.6 0.1 reshape_tile.3
  2.7 0.5 compare_select_fusion.slot_ref
  3.3 91.6 %exchange.1 = (f32[4,2,4,32,1024]{4,3,2,1,0:T(8,128)}, f32[4,2,2,8,1024]{4,3,2,1,0:T(8,128)}, s32[8,8,128]{2,1,0:T(8,128)}) custom-call(bf16[32,65536]{1,0:T(8,128)(2,1)} %jac_ref.1, s32[1,128]{1,0:T(1,128)} %compare_select_fusion.slot_ref, s32[2]{0:T(128)} %pad_add_fusion.place_ref), custom_call_target="tpu_custom_call" | custom-call | tf_op jit(solution)/shard_map/exchange/pallas_call | solution.py:349
  94.8 0.8 dynamic-slice_reduce_fusion.1
  95.6 0.1 reshape.89
  95.7 0.1 eq.34
  95.8 0.7 compare_convert_fusion.pick_ref
  96.5 76.4 %reduce.9 = (f32[8,4,2,2,8,1024]{5,4,3,2,1,0:T(8,128)}, f32[32,1024]{1,0:T(8,128)}) custom-call(f32[4,2,2,8,1024]{4,3,2,1,0:T(8,128)} %get-tuple-element.10.p_ref, f32[4,2,4,32,1024]{4,3,2,1,0:T(8,128)} %get-tuple-element.11.c_ref, bf16[128,256]{1,0:T(8,128)(2,1)} %compare_convert_fusion.pick_ref, s32[2]{0:T(128)} %pad_add_fusion.place_ref, f32[1]{0:T(128)S(6)} %copy.6.shift_ref), custom_call_target="tpu_custom_call" | custom-call | tf_op jit(solution)/shard_map/reduce/pallas_call | solution.py:528
  172.9 42.0 %factor.1 = f32[32,1024]{1,0:T(8,128)} custom-call(f32[1024,1024]{1,0:T(8,128)} %bitcast.8, f32[32,1024]{1,0:T(8,128)} %get-tuple-element.14.g_ref), custom_call_target="tpu_custom_call" | custom-call | tf_op jit(solution)/shard_map/factor/pallas_call | solution.py:123
  (2 shorter events, 0.0 us)
where the time goes:
time: 215 us
  Pallas kernels  210 us (98%)
    pallas_call x1, Pallas kernels, exchanged(): pl.pallas_call(exchange_kernel, out_shape=(jax.ShapeDtypeStruct((Y, 2, X,...  91.6 us
    pallas_call x1, Pallas kernels, reduced(): pl.pallas_call(reduce_kernel, out_shape=(jax.ShapeDtypeStruct((Z, Y, 2, 2...  76.4 us
    pallas_call x1, Pallas kernels, solved(): pl.pallas_call(factor_kernel, out_shape=jax.ShapeDtypeStruct(rows.shape,...  42 us

commit v1 on v0

--- a/solution.py
+++ b/solution.py
@@ -370,7 +370,7 @@
 
 def reduce_kernel(p_ref, c_ref, pick_ref, place_ref, shift_ref, o_ref, g_ref,
                   got, piece, sib, acc, first0, first1, acc0, acc1, second0, second1,
-                  part, column_rows, chosen, third,
+                  column_rows, chosen, third,
                   ps, pr, zs, zr, xs, xr, ys, yr, ys2, yr2, xs2, xr2, cs, cr,
                   ss, sr, s0, r0, s1, r1, t0, q0, t1, q1, us, ur, vs, vr):
     samp, z, x = here()
@@ -381,7 +381,12 @@
     meet([peer for _, peer in column] + [peer for _, _, peer in plane])
     n = p_ref.shape[4]
     wide = n // 2
-    low, high = pl.ds(0, wide), pl.ds(wide, wide)
+    narrow = wide // X
+    low = pl.ds(0, wide)
+
+    def share(u, half):
+        return pl.ds(pl.multiple_of(half * wide + u * narrow, narrow), narrow)
+
     order = (2, 1, 3)
     sends = []
 
@@ -420,7 +425,7 @@
             start(copy_to(acc.at[v, :, :, low], first0.at[d], s0.at[d], r0.at[d], peer))
     for d in order:
         u, peer = along(d)
-        start(copy_to(acc.at[:, u, :, high], first1.at[d], s1.at[d], r1.at[d], peer))
+        start(copy_to(acc.at[:, :, :, share(u, 1)], first1.at[d], s1.at[d], r1.at[d], peer))
 
     total = p_ref[y, core, xh, :, cols(xl)]
     for ds, dx, _ in plane:
@@ -448,10 +453,10 @@
     acc0[...] = acc[y, :, :, low] + first0[1] + first0[2] + first0[3]
     for d in order:
         u, peer = along(d)
-        start(copy_to(acc0.at[u], second0.at[d], t0.at[d], q0.at[d], peer))
+        start(copy_to(acc0.at[:, :, share(u, 0)], second0.at[d], t0.at[d], q0.at[d], peer))
     for d in order:
         arrived(first1.at[d], s1.at[d], r1.at[d])
-    acc1[...] = acc[:, x, :, high] + first1[1] + first1[2] + first1[3]
+    acc1[...] = acc[:, :, :, share(x, 1)] + first1[1] + first1[2] + first1[3]
     for d in order:
         v, peer = up(d)
         start(copy_to(acc1.at[v], second1.at[d], t1.at[d], q1.at[d], peer))
@@ -473,11 +478,31 @@
     for d in order:
         arrived(second0.at[d], t0.at[d], q0.at[d])
         arrived(second1.at[d], t1.at[d], q1.at[d])
-    part[:, low] = acc0[x] + second0[1] + second0[2] + second0[3]
-    part[:, high] = acc1[y] + second1[1] + second1[2] + second1[3]
-    column_rows[z] = part[...]
-    for dz, peer in column:
-        start(copy_to(part, column_rows.at[z], us.at[dz], ur.at[dz], peer))
+    column_rows[z, :, :, pl.ds(0, narrow)] = (
+        acc0[:, :, share(x, 0)] + second0[1] + second0[2] + second0[3])
+    column_rows[z, :, :, pl.ds(narrow, narrow)] = acc1[y] + second1[1] + second1[2] + second1[3]
+
+    def half_of(owner, h):
+        return column_rows.at[owner, pl.ds(h * (X // 2), X // 2)]
+
+    def hop(s):
+        for h in range(2):
+            for d in range(2):
+                if s > 0:
+                    came(d, s - 1, h)
+                if s < 3 or h == d:
+                    owner = wrapped(z - s, Z) if d == 0 else wrapped(z + s, Z)
+                    to = at(samp, wrapped(z + 1, Z) if d == 0 else wrapped(z - 1, Z), x)
+                    ref = half_of(owner, h)
+                    start(copy_to(ref, ref, us.at[d, s, h], ur.at[d, s, h], to))
+
+    def came(d, s, h):
+        owner = wrapped(z - 1 - s, Z) if d == 0 else wrapped(z + 1 + s, Z)
+        arrived(half_of(owner, h), us.at[d, s, h], ur.at[d, s, h])
+
+    hop(0)
+    hop(1)
+    hop(2)
 
     for d in order:
         u = wrapped(x - d, X)
@@ -490,10 +515,11 @@
         ref = o_ref.at[:, v, core]
         start(copy_to(ref, ref, cs.at[d], cr.at[d], sibling))
 
-    for dz, _ in column:
-        arrived(column_rows.at[wrapped(z - dz, Z)], us.at[dz], ur.at[dz])
-    rest = column_rows[...].reshape(pick_ref.shape[1], n)
-    moved = jnp.zeros((pick_ref.shape[0], n), jnp.float32)
+    hop(3)
+    for d in range(2):
+        came(d, 3, d)
+    rest = column_rows[...].reshape(pick_ref.shape[1], 2 * narrow)
+    moved = jnp.zeros((pick_ref.shape[0], 2 * narrow), jnp.float32)
     for _ in range(3):
         head = rest.astype(jnp.bfloat16)
         rest = rest - head.astype(jnp.float32)
@@ -505,13 +531,21 @@
         u, peer = along(d)
         start(copy_to(chosen.at[u], third.at[d], vs.at[d], vr.at[d], peer))
     width = chosen.shape[1]
-    position = lax.broadcasted_iota(jnp.int32, (width, n), 0) + (z * X + x) * width
-    column_id = lax.broadcasted_iota(jnp.int32, (width, n), 1)
-    on_pivot = jnp.where(position == lax.rem(column_id + place_ref[1], n), shift_ref[0], 0.0)
-    on_pivot = jnp.where(place_ref[0] == samp, on_pivot, 0.0)
+    position = lax.broadcasted_iota(jnp.int32, (width, narrow), 0) + (z * X + x) * width
+
+    def finish(u, values):
+        for half in range(2):
+            to = share(u, half)
+            piece_columns = lax.broadcasted_iota(jnp.int32, (width, narrow), 1)
+            piece_columns = piece_columns + (half * wide + u * narrow)
+            added = jnp.where(position == lax.rem(piece_columns + place_ref[1], n), shift_ref[0], 0.0)
+            added = jnp.where(place_ref[0] == samp, added, 0.0)
+            g_ref[:, to] = values[:, half * narrow : half * narrow + narrow] / SAMPLES + added
+
+    finish(x, chosen[x])
     for d in order:
         arrived(third.at[d], vs.at[d], vr.at[d])
-    g_ref[...] = (chosen[x] + third[1] + third[2] + third[3]) / SAMPLES + on_pivot
+        finish(wrapped(x - d, X), third[d])
     for d in range(Y):
         arrived(o_ref.at[:, wrapped(y - d, Y), 1 - core], cs.at[d], cr.at[d])
     for copy in sends:
@@ -534,15 +568,15 @@
         scratch_shapes=[
             pltpu.VMEM((GROUPS, X, 8, wide), f32), pltpu.VMEM((8, wide), f32),
             pltpu.VMEM((Y, X, rows, n), f32), pltpu.VMEM((Y, X, rows, n), f32),
-            pltpu.VMEM((Y, X, rows, wide), f32), pltpu.VMEM((X, Y, rows, wide), f32),
-            pltpu.VMEM((X, rows, wide), f32), pltpu.VMEM((Y, rows, wide), f32),
-            pltpu.VMEM((X, rows, wide), f32), pltpu.VMEM((Y, rows, wide), f32),
-            pltpu.VMEM((rows, n), f32), pltpu.VMEM((Z, rows, n), f32),
-            pltpu.VMEM((X, rows, n), f32), pltpu.VMEM((X, rows, n), f32),
+            pltpu.VMEM((Y, X, rows, wide), f32), pltpu.VMEM((X, Y, X, rows, wide // X), f32),
+            pltpu.VMEM((X, rows, wide), f32), pltpu.VMEM((Y, X, rows, wide // X), f32),
+            pltpu.VMEM((X, X, rows, wide // X), f32), pltpu.VMEM((Y, X, rows, wide // X), f32),
+            pltpu.VMEM((Z, X, rows, n // X), f32),
+            pltpu.VMEM((X, rows, n // X), f32), pltpu.VMEM((X, rows, n // X), f32),
             dma((GROUPS, X)), dma((GROUPS, X)), dma((Z,)), dma((Z,)),
             dma((4,)), dma((4,)), dma((4,)), dma((4,)),
             dma((4, 2)), dma((4, 2)), dma((4,)), dma((4,)), dma((4,)), dma((4,)),
-        ] + [dma((4,))] * 10 + [dma((Z,)), dma((Z,)), dma((4,)), dma((4,))],
+        ] + [dma((4,))] * 10 + [dma((2, 4, 2)), dma((2, 4, 2)), dma((4,)), dma((4,))],
         compiler_params=pltpu.CompilerParams(collective_id=1, has_side_effects=True),
         name="reduce",
     )(part, partial, pick, place, shift)
@@ -561,10 +595,8 @@
     place = jnp.stack([pivot_group, rotation])
     partial, pivot_part, slots = exchanged(jacobian, padded, place)
     own_slots = lax.dynamic_index_in_dim(slots, lax.axis_index("samp"), 1, keepdims=False)
-    sources = own_slots.reshape(-1, X, width)
-    sources = lax.dynamic_index_in_dim(sources, lax.axis_index("x"), 1, keepdims=False)
     target = lax.axis_index("z") * band + jnp.arange(band, dtype=jnp.int32)
-    pick = (target[:, None] == sources.reshape(1, -1)).astype(jnp.bfloat16)
+    pick = (target[:, None] == own_slots.reshape(1, -1)).astype(jnp.bfloat16)
     block, my_rows = reduced(pivot_part, partial, pick, place, shift_value)
     return solved(my_rows, block)
 

time: 215 us -> 202 us (0.940)
  Pallas kernels: 210 us -> 197 us
    pallas_call x1, Pallas kernels: 76.4 us -> 63 us  [reduced(): pl.pallas_call(reduce_kernel, out_shape=(jax.ShapeDtypeStruct((Z, Y, 2, 2...]
where the time goes in v1:
time: 202 us; the launch traced here: 201 us
  Pallas kernels  197 us (98%)
    pallas_call x1, Pallas kernels, exchanged(): pl.pallas_call(exchange_kernel, out_shape=(jax.ShapeDtypeStruct((Y, 2, X,...  91.6 us
    pallas_call x1, Pallas kernels, reduced(): pl.pallas_call(reduce_kernel, out_shape=(jax.ShapeDtypeStruct((Z, Y, 2, 2...  63 us
    pallas_call x1, Pallas kernels, solved(): pl.pallas_call(factor_kernel, out_shape=jax.ShapeDtypeStruct(rows.shape,...  42.1 us

profile of v1, /device:TPU:2, one launch (start us, length us, event | category | flops | bytes accessed | tf_op | source)
XLA Modules:
  0.0 201.4 jit_solution(6009868323275439763)
XLA Ops:
  1.3 0.6 pad_add_fusion.place_ref
  1.9 0.7 tile.2
  2.6 0.1 reshape_tile.3
  2.7 0.5 compare_select_fusion.slot_ref
  3.2 91.6 %exchange.1 = (f32[4,2,4,32,1024]{4,3,2,1,0:T(8,128)}, f32[4,2,2,8,1024]{4,3,2,1,0:T(8,128)}, s32[8,8,128]{2,1,0:T(8,128)}) custom-call(bf16[32,65536]{1,0:T(8,128)(2,1)} %jac_ref.1, s32[1,128]{1,0:T(1,128)} %compare_select_fusion.slot_ref, s32[2]{0:T(128)} %pad_add_fusion.place_ref), custom_call_target="tpu_custom_call" | custom-call | tf_op jit(solution)/shard_map/exchange/pallas_call | solution.py:349
  94.8 0.8 constant_dynamic-slice_fusion
  95.5 0.8 compare_convert_fusion.pick_ref
  96.4 63.0 %reduce.1 = (f32[8,4,2,2,8,1024]{5,4,3,2,1,0:T(8,128)}, f32[32,1024]{1,0:T(8,128)}) custom-call(f32[4,2,2,8,1024]{4,3,2,1,0:T(8,128)} %get-tuple-element.10.p_ref, f32[4,2,4,32,1024]{4,3,2,1,0:T(8,128)} %get-tuple-element.11.c_ref, bf16[128,1024]{1,0:T(8,128)(2,1)} %compare_convert_fusion.pick_ref, s32[2]{0:T(128)} %pad_add_fusion.place_ref, f32[1]{0:T(128)S(6)} %copy.6.shift_ref), custom_call_target="tpu_custom_call" | custom-call | tf_op jit(solution)/shard_map/reduce/pallas_call | solution.py:562
  159.4 42.1 %factor.1 = f32[32,1024]{1,0:T(8,128)} custom-call(f32[1024,1024]{1,0:T(8,128)} %bitcast.9, f32[32,1024]{1,0:T(8,128)} %get-tuple-element.14.g_ref), custom_call_target="tpu_custom_call" | custom-call | tf_op jit(solution)/shard_map/factor/pallas_call | solution.py:123
  (1 shorter events, 0.0 us)
